TPU v7x, 256 devices: a whole 4x4x8 slice. The times are simulated.
256 devices in a mesh: dom: 64 (over x, z, core), slab: 4 (over y).
Axes of the slice: x: 4, y: 4, z: 8, core: 2. Of those that a mesh axis runs over, the one named last changes fastest.
Arguments:
- logperm: float32 [256, 16, 64, 128], P('dom', 'slab'), may hold values from -4.2 to 4.2
- source: float32 [16, 64, 128], P('slab'), may hold values from -6 to 6
- observed: float32 [16, 64, 128], P('slab'), may hold values from -1.2 to 1.2
- brownian: float32 [256, 256], replicated, may hold values from -6 to 6
Outputs:
- particles_next: float32 [256, 16, 64, 128], P('dom', 'slab')
All inputs are finite; a program needn't handle non-finite values.
Results may differ from a plain program's by a relative error of at most 0.0003.
Values sent between devices are 32-bit elements; how exact they have to be, the bound alone decides.
No kernel may reach another device: no remote copies, remote signals or barrier semaphores. Data moves between devices by JAX's collectives and lax.ppermute only.
A program may use at most 64 MiB of HBM per device.

v0:
```python
import math
import jax
import jax.numpy as jnp
from jax import lax
from jax.sharding import PartitionSpec as P

SWEEPS = 8
misfit_weight = 1000.0


def with_halo(block, sides, width):
    for axis, dim in sides:
        count = lax.axis_size(axis)
        forward = [(i, i + 1) for i in range(count - 1)]
        backward = [(target, source) for source, target in forward]
        low = lax.ppermute(
            lax.slice_in_dim(block, block.shape[dim] - width, None, axis=dim), axis, forward
        )
        high = lax.ppermute(lax.slice_in_dim(block, 0, width, axis=dim), axis, backward)
        block = jnp.concatenate([low, block, high], axis=dim)
    return block


def neighbor_sum(core, below, above, fill):
    pad_y = jnp.pad(core, ((0, 0), (0, 0), (1, 1), (0, 0)), constant_values=fill)
    pad_z = jnp.pad(core, ((0, 0), (0, 0), (0, 0), (1, 1)), constant_values=fill)
    return below + above + pad_y[:, :, :-2] + pad_y[:, :, 2:] + pad_z[..., :-2] + pad_z[..., 2:]


def grad_field(e_core, e_below, e_above, p_core, p_below, p_above, q_core, q_below, q_above):
    summed = e_below * (p_core - p_below) * (q_core - q_below) + e_above * (p_core - p_above) * (
        q_core - q_above
    )
    for dimension in (2, 3):
        padding = [(0, 0), (0, 0), (0, 0), (0, 0)]
        padding[dimension] = (1, 1)
        e_pad = jnp.pad(e_core, padding, constant_values=1.0)
        p_pad = jnp.pad(p_core, padding)
        q_pad = jnp.pad(q_core, padding)
        extent = e_core.shape[dimension]
        for offset in (0, 2):
            e_near = lax.slice_in_dim(e_pad, offset, offset + extent, axis=dimension)
            p_near = lax.slice_in_dim(p_pad, offset, offset + extent, axis=dimension)
            q_near = lax.slice_in_dim(q_pad, offset, offset + extent, axis=dimension)
            summed = summed + e_near * (p_core - p_near) * (q_core - q_near)
    return -0.5 * e_core * summed


def on_device(logperm, source, observed, brownian):
    particles, width, rows_y, depth_z = logperm.shape
    slabs = lax.axis_size("slab")
    cells = width * slabs * rows_y * depth_z
    extended = with_halo(logperm, (("slab", 1),), 1)
    e_ext = jnp.exp(0.5 * extended)
    e_core = e_ext[:, 1:-1]
    inverse = 1.0 / neighbor_sum(e_core, e_ext[:, :-2], e_ext[:, 2:], 1.0)

    def relax_rim(rhs):
        value = inverse * rhs
        for sweep_index in range(SWEEPS - 1):
            bordered = with_halo(value, (("slab", 1),), 1)
            value = inverse * (
                rhs + e_core * neighbor_sum(value, bordered[:, :-2], bordered[:, 2:], 0.0)
            )
        return value / e_core

    pressure = relax_rim(source[None])
    misfit = misfit_weight * (pressure - observed[None])
    adjoint = relax_rim(misfit)
    states = with_halo(jnp.stack([pressure, adjoint]), (("slab", 2),), 1)
    gradient = grad_field(
        e_core,
        e_ext[:, :-2],
        e_ext[:, 2:],
        pressure,
        states[0][:, :-2],
        states[0][:, 2:],
        adjoint,
        states[1][:, :-2],
        states[1][:, 2:],
    )
    g_flat = gradient.reshape(particles, -1)
    u_cells, g_cells = (
        lax.all_to_all(
            logperm.reshape(particles, -1), "dom", split_axis=1, concat_axis=0, tiled=True
        ),
        lax.all_to_all(g_flat, "dom", split_axis=1, concat_axis=0, tiled=True),
    )
    ensemble = u_cells.shape[0]
    centre = jnp.mean(u_cells, axis=0, keepdims=True)
    spread = u_cells - centre
    partial_gram = lax.dot_general(
        spread,
        g_cells,
        (((1,), (1,)), ((), ())),
        precision=lax.Precision.HIGHEST,
        preferred_element_type=jnp.float32,
    )
    gram = lax.psum(partial_gram, ("dom", "slab"))
    step_size = ensemble / (4.0 * (cells + 1))
    mixing = -(step_size / ensemble) * gram + math.sqrt(2.0 * step_size / ensemble) * brownian
    moved = (
        centre
        + 1.25 * spread
        + lax.dot_general(
            mixing,
            spread,
            (((0,), (0,)), ((), ())),
            precision=lax.Precision.HIGHEST,
            preferred_element_type=jnp.float32,
        )
    )
    returned = lax.all_to_all(moved, "dom", split_axis=0, concat_axis=1, tiled=True)
    return returned.reshape(logperm.shape)


def solution(mesh):
    return jax.shard_map(
        on_device,
        mesh=mesh,
        in_specs=(P("dom", "slab", None, None), P("slab", None, None), P("slab", None, None), P()),
        out_specs=P("dom", "slab", None, None),
        check_vma=False,
    )
```

profile of v0, /device:TPU:1, one launch (start us, length us, event | category | flops | bytes accessed | tf_op | source)
XLA Modules:
  0.0 498.0 jit_solution(12891519340523834035)
XLA Ops:
  7.6 4.0 collective-permute-start
  13.7 3.6 collective-permute-done.1
  18.9 3.2 collective-permute-start.2
  24.1 3.8 collective-permute-done.3
  28.3 2.9 collective-permute-start.4
  33.1 3.8 collective-permute-done.5
  37.3 2.2 collective-permute-start.6
  41.5 3.8 collective-permute-done.7
  49.5 3.8 collective-permute-done.9
  57.6 3.8 collective-permute-done.11
  61.8 2.1 collective-permute-start.12
  66.1 4.1 collective-permute-done.13
  75.3 3.9 collective-permute-done.15
  79.7 2.1 collective-permute-start.16
  84.2 3.8 collective-permute-done.17
  88.4 2.2 collective-permute-start.18
  92.6 3.8 collective-permute-done.19
  96.9 2.2 collective-permute-start.20
  101.0 3.8 collective-permute-done.21
  105.3 2.2 collective-permute-start.22
  109.4 3.8 collective-permute-done.23
  113.7 1.9 collective-permute-start.24
  117.5 3.8 collective-permute-done.25
  125.7 3.8 collective-permute-done.27
  133.8 3.9 collective-permute-done.29
  139.1 2.6 collective-permute-start.30
  144.2 28.9 %all-to-all-start = ((f32[4,64,512]{2,0,1:T(4,128)}), f32[4,64,512]{2,0,1:T(4,128)S(1)}, u32[]{:S(2)}, u32[]{:S(2)}) async-start(f32[4,64,512]{2,0,1:T(4,128)} %copy.7), calls=%async_computation | async-start | bytes 1048576 | tf_op jit(solution)/shard_map/all_to_all | solution.py:84
  176.8 13.7 %all-to-all-done = f32[4,64,512]{2,0,1:T(4,128)S(1)} async-done(((f32[4,64,512]{2,0,1:T(4,128)}), f32[4,64,512]{2,0,1:T(4,128)S(1)}, u32[]{:S(2)}, u32[]{:S(2)}) %all-to-all-start) | async-done | bytes 524320 | tf_op jit(solution)/shard_map/all_to_all | solution.py:84
  190.4 6.3 %all-to-all-start.1 = ((f32[4,64,512]{2,0,1:T(4,128)}), f32[4,64,512]{2,0,1:T(4,128)S(1)}, u32[]{:S(2)}, u32[]{:S(2)}) async-start(f32[4,64,512]{2,0,1:T(4,128)} %copy.8), calls=%async_computation.1 | async-start | bytes 1048576 | tf_op jit(solution)/shard_map/all_to_all | solution.py:87
  197.2 16.9 %all-to-all-done.1 = f32[4,64,512]{2,0,1:T(4,128)S(1)} async-done(((f32[4,64,512]{2,0,1:T(4,128)}), f32[4,64,512]{2,0,1:T(4,128)S(1)}, u32[]{:S(2)}, u32[]{:S(2)}) %all-to-all-start.1) | async-done | bytes 524320 | tf_op jit(solution)/shard_map/all_to_all | solution.py:87
  215.8 245.4 %all-reduce.36.cloned.1.call-done = f32[256,256]{1,0:T(8,128)} async-done(((f32[256,256]{1,0:T(8,128)}), f32[256,256]{1,0:T(8,128)}) %all-reduce.36.cloned.1.call-update) | async-done | bytes 262160 | tf_op jit(solution)/shard_map/psum | solution.py:99
  462.9 27.3 %all_to_all.54 = f32[64,4,512]{2,1,0:T(4,128)S(1)} all-to-all(f32[64,4,512]{2,1,0:T(4,128)S(1)} %all_to_all.48), channel_id=1, replica_groups=mesh['dom'=64,'slab'=4] {'dom'}, dimensions={0} | all-to-all | bytes 1048576 | tf_op jit(solution)/shard_map/all_to_all | solution.py:113
  (99 shorter events, 60.8 us)
Async XLA Ops:
  7.6 6.2 %collective-permute-start = (f32[4,1,64,128]{3,2,1,0:T(8,128)S(1)}, f32[4,1,64,128]{3,2,1,0:T(8,128)S(1)}, u32[]{:S(2)}, u32[]{:S(2)}) collective-permute-start(f32[4,1,64,128]{3,2,1,0:T(8,128)S(1)} %get-tuple-element.41), channel_id=1, source_target_pairs={{0,1},{1,2},{2,3},{4,5},{5,6},{6,7},{8,9},{9,10},{10,11},{12,13},{... | collective-permute-start | bytes 393224 | tf_op jit(solution)/shard_map/ppermute | solution.py:16
  11.6 5.7 %collective-permute-start.1 = (f32[4,1,64,128]{3,2,1,0:T(8,128)S(1)}, f32[4,1,64,128]{3,2,1,0:T(8,128)S(1)}, u32[]{:S(2)}, u32[]{:S(2)}) collective-permute-start(f32[4,1,64,128]{3,2,1,0:T(8,128)S(1)} %get-tuple-element.42), channel_id=1, source_target_pairs={{1,0},{2,1},{3,2},{5,4},{6,5},{7,6},{9,8},{10,9},{11,10},{13,12},{... | collective-permute-start | bytes 393224 | tf_op jit(solution)/shard_map/ppermute | solution.py:19
  18.9 5.1 %collective-permute-start.2 = (f32[4,1,64,128]{3,2,1,0:T(8,128)S(1)}, f32[4,1,64,128]{3,2,1,0:T(8,128)S(1)}, u32[]{:S(2)}, u32[]{:S(2)}) collective-permute-start(f32[4,1,64,128]{3,2,1,0:T(8,128)S(1)} %get-tuple-element.39), channel_id=1, source_target_pairs={{0,1},{1,2},{2,3},{4,5},{5,6},{6,7},{8,9},{9,10},{10,11},{12,13},{... | collective-permute-start | bytes 393224 | tf_op jit(solution)/shard_map/ppermute | solution.py:16
  22.2 5.7 %collective-permute-start.3 = (f32[4,1,64,128]{3,2,1,0:T(8,128)S(1)}, f32[4,1,64,128]{3,2,1,0:T(8,128)S(1)}, u32[]{:S(2)}, u32[]{:S(2)}) collective-permute-start(f32[4,1,64,128]{3,2,1,0:T(8,128)S(1)} %get-tuple-element.40), channel_id=1, source_target_pairs={{1,0},{2,1},{3,2},{5,4},{6,5},{7,6},{9,8},{10,9},{11,10},{13,12},{... | collective-permute-start | bytes 393224 | tf_op jit(solution)/shard_map/ppermute | solution.py:19
  28.3 4.8 collective-permute-start.4
  31.2 5.7 %collective-permute-start.5 = (f32[4,1,64,128]{3,2,1,0:T(8,128)S(1)}, f32[4,1,64,128]{3,2,1,0:T(8,128)S(1)}, u32[]{:S(2)}, u32[]{:S(2)}) collective-permute-start(f32[4,1,64,128]{3,2,1,0:T(8,128)S(1)} %get-tuple-element.38), channel_id=1, source_target_pairs={{1,0},{2,1},{3,2},{5,4},{6,5},{7,6},{9,8},{10,9},{11,10},{13,12},{... | collective-permute-start | bytes 393224 | tf_op jit(solution)/shard_map/ppermute | solution.py:19
  37.3 4.1 collective-permute-start.6
  39.6 5.7 %collective-permute-start.7 = (f32[4,1,64,128]{3,2,1,0:T(8,128)S(1)}, f32[4,1,64,128]{3,2,1,0:T(8,128)S(1)}, u32[]{:S(2)}, u32[]{:S(2)}) collective-permute-start(f32[4,1,64,128]{3,2,1,0:T(8,128)S(1)} %get-tuple-element.36), channel_id=1, source_target_pairs={{1,0},{2,1},{3,2},{5,4},{6,5},{7,6},{9,8},{10,9},{11,10},{13,12},{... | collective-permute-start | bytes 393224 | tf_op jit(solution)/shard_map/ppermute | solution.py:19
  47.6 5.7 %collective-permute-start.9 = (f32[4,1,64,128]{3,2,1,0:T(8,128)S(1)}, f32[4,1,64,128]{3,2,1,0:T(8,128)S(1)}, u32[]{:S(2)}, u32[]{:S(2)}) collective-permute-start(f32[4,1,64,128]{3,2,1,0:T(8,128)S(1)} %get-tuple-element.34), channel_id=1, source_target_pairs={{1,0},{2,1},{3,2},{5,4},{6,5},{7,6},{9,8},{10,9},{11,10},{13,12},{... | collective-permute-start | bytes 393224 | tf_op jit(solution)/shard_map/ppermute | solution.py:19
  53.7 3.9 collective-permute-start.10
  55.7 5.7 %collective-permute-start.11 = (f32[4,1,64,128]{3,2,1,0:T(8,128)S(1)}, f32[4,1,64,128]{3,2,1,0:T(8,128)S(1)}, u32[]{:S(2)}, u32[]{:S(2)}) collective-permute-start(f32[4,1,64,128]{3,2,1,0:T(8,128)S(1)} %get-tuple-element.32), channel_id=1, source_target_pairs={{1,0},{2,1},{3,2},{5,4},{6,5},{7,6},{9,8},{10,9},{11,10},{13,12},{... | collective-permute-start | bytes 393224 | tf_op jit(solution)/shard_map/ppermute | solution.py:19
  61.8 4.3 collective-permute-start.12
  63.9 6.3 %collective-permute-start.13 = (f32[4,1,64,128]{3,2,1,0:T(8,128)S(1)}, f32[4,1,64,128]{3,2,1,0:T(8,128)S(1)}, u32[]{:S(2)}, u32[]{:S(2)}) collective-permute-start(f32[4,1,64,128]{3,2,1,0:T(8,128)S(1)} %get-tuple-element.30), channel_id=1, source_target_pairs={{1,0},{2,1},{3,2},{5,4},{6,5},{7,6},{9,8},{10,9},{11,10},{13,12},{... | collective-permute-start | bytes 393224 | tf_op jit(solution)/shard_map/ppermute | solution.py:19
  70.6 4.7 collective-permute-start.14
  72.3 7.0 %collective-permute-start.15 = (f32[4,1,64,128]{3,2,1,0:T(8,128)S(1)}, f32[4,1,64,128]{3,2,1,0:T(8,128)S(1)}, u32[]{:S(2)}, u32[]{:S(2)}) collective-permute-start(f32[4,1,64,128]{3,2,1,0:T(8,128)S(1)} %get-tuple-element.28), channel_id=1, source_target_pairs={{1,0},{2,1},{3,2},{5,4},{6,5},{7,6},{9,8},{10,9},{11,10},{13,12},{... | collective-permute-start | bytes 393224 | tf_op jit(solution)/shard_map/ppermute | solution.py:19
  79.7 4.4 collective-permute-start.16
  81.9 6.1 %collective-permute-start.17 = (f32[4,1,64,128]{3,2,1,0:T(8,128)S(1)}, f32[4,1,64,128]{3,2,1,0:T(8,128)S(1)}, u32[]{:S(2)}, u32[]{:S(2)}) collective-permute-start(f32[4,1,64,128]{3,2,1,0:T(8,128)S(1)} %get-tuple-element.26), channel_id=1, source_target_pairs={{1,0},{2,1},{3,2},{5,4},{6,5},{7,6},{9,8},{10,9},{11,10},{13,12},{... | collective-permute-start | bytes 393224 | tf_op jit(solution)/shard_map/ppermute | solution.py:19
  88.4 4.2 collective-permute-start.18
  90.7 5.7 %collective-permute-start.19 = (f32[4,1,64,128]{3,2,1,0:T(8,128)S(1)}, f32[4,1,64,128]{3,2,1,0:T(8,128)S(1)}, u32[]{:S(2)}, u32[]{:S(2)}) collective-permute-start(f32[4,1,64,128]{3,2,1,0:T(8,128)S(1)} %get-tuple-element.24), channel_id=1, source_target_pairs={{1,0},{2,1},{3,2},{5,4},{6,5},{7,6},{9,8},{10,9},{11,10},{13,12},{... | collective-permute-start | bytes 393224 | tf_op jit(solution)/shard_map/ppermute | solution.py:19
  96.9 4.1 collective-permute-start.20
  99.1 5.7 %collective-permute-start.21 = (f32[4,1,64,128]{3,2,1,0:T(8,128)S(1)}, f32[4,1,64,128]{3,2,1,0:T(8,128)S(1)}, u32[]{:S(2)}, u32[]{:S(2)}) collective-permute-start(f32[4,1,64,128]{3,2,1,0:T(8,128)S(1)} %get-tuple-element.22), channel_id=1, source_target_pairs={{1,0},{2,1},{3,2},{5,4},{6,5},{7,6},{9,8},{10,9},{11,10},{13,12},{... | collective-permute-start | bytes 393224 | tf_op jit(solution)/shard_map/ppermute | solution.py:19
  105.3 4.1 collective-permute-start.22
  107.5 5.7 %collective-permute-start.23 = (f32[4,1,64,128]{3,2,1,0:T(8,128)S(1)}, f32[4,1,64,128]{3,2,1,0:T(8,128)S(1)}, u32[]{:S(2)}, u32[]{:S(2)}) collective-permute-start(f32[4,1,64,128]{3,2,1,0:T(8,128)S(1)} %get-tuple-element.20), channel_id=1, source_target_pairs={{1,0},{2,1},{3,2},{5,4},{6,5},{7,6},{9,8},{10,9},{11,10},{13,12},{... | collective-permute-start | bytes 393224 | tf_op jit(solution)/shard_map/ppermute | solution.py:19
  113.7 3.9 collective-permute-start.24
  115.6 5.7 %collective-permute-start.25 = (f32[4,1,64,128]{3,2,1,0:T(8,128)S(1)}, f32[4,1,64,128]{3,2,1,0:T(8,128)S(1)}, u32[]{:S(2)}, u32[]{:S(2)}) collective-permute-start(f32[4,1,64,128]{3,2,1,0:T(8,128)S(1)} %get-tuple-element.18), channel_id=1, source_target_pairs={{1,0},{2,1},{3,2},{5,4},{6,5},{7,6},{9,8},{10,9},{11,10},{13,12},{... | collective-permute-start | bytes 393224 | tf_op jit(solution)/shard_map/ppermute | solution.py:19
  123.8 5.7 %collective-permute-start.27 = (f32[4,1,64,128]{3,2,1,0:T(8,128)S(1)}, f32[4,1,64,128]{3,2,1,0:T(8,128)S(1)}, u32[]{:S(2)}, u32[]{:S(2)}) collective-permute-start(f32[4,1,64,128]{3,2,1,0:T(8,128)S(1)} %get-tuple-element.16), channel_id=1, source_target_pairs={{1,0},{2,1},{3,2},{5,4},{6,5},{7,6},{9,8},{10,9},{11,10},{13,12},{... | collective-permute-start | bytes 393224 | tf_op jit(solution)/shard_map/ppermute | solution.py:19
  131.9 5.8 %collective-permute-start.29 = (f32[4,1,64,128]{3,2,1,0:T(8,128)S(1)}, f32[4,1,64,128]{3,2,1,0:T(8,128)S(1)}, u32[]{:S(2)}, u32[]{:S(2)}) collective-permute-start(f32[4,1,64,128]{3,2,1,0:T(8,128)S(1)} %get-tuple-element.14), channel_id=1, source_target_pairs={{1,0},{2,1},{3,2},{5,4},{6,5},{7,6},{9,8},{10,9},{11,10},{13,12},{... | collective-permute-start | bytes 393224 | tf_op jit(solution)/shard_map/ppermute | solution.py:19
  139.1 34.0 %collective-permute-start.30 = (f32[2,4,1,64,128]{4,3,2,1,0:T(8,128)}, f32[2,4,1,64,128]{4,3,2,1,0:T(8,128)}, u32[]{:S(2)}, u32[]{:S(2)}) collective-permute-start(f32[2,4,1,64,128]{4,3,2,1,0:T(8,128)} %get-tuple-element.11), channel_id=1, source_target_pairs={{0,1},{1,2},{2,3},{4,5},{5,6},{6,7},{8,9},{9,10},{10,11},{12,13},{... | collective-permute-start | bytes 786440 | tf_op jit(solution)/shard_map/ppermute | solution.py:16
  141.7 31.4 %collective-permute-start.31 = (f32[2,4,1,64,128]{4,3,2,1,0:T(8,128)}, f32[2,4,1,64,128]{4,3,2,1,0:T(8,128)}, u32[]{:S(2)}, u32[]{:S(2)}) collective-permute-start(f32[2,4,1,64,128]{4,3,2,1,0:T(8,128)} %get-tuple-element.12), channel_id=1, source_target_pairs={{1,0},{2,1},{3,2},{5,4},{6,5},{7,6},{9,8},{10,9},{11,10},{13,12},{... | collective-permute-start | bytes 786440 | tf_op jit(solution)/shard_map/ppermute | solution.py:19
  144.2 46.2 %all-to-all-start = ((f32[4,64,512]{2,0,1:T(4,128)}), f32[4,64,512]{2,0,1:T(4,128)S(1)}, u32[]{:S(2)}, u32[]{:S(2)}) async-start(f32[4,64,512]{2,0,1:T(4,128)} %copy.7), calls=%async_computation | async-start | bytes 1048576 | tf_op jit(solution)/shard_map/all_to_all | solution.py:84
  190.4 23.6 %all-to-all-start.1 = ((f32[4,64,512]{2,0,1:T(4,128)}), f32[4,64,512]{2,0,1:T(4,128)S(1)}, u32[]{:S(2)}, u32[]{:S(2)}) async-start(f32[4,64,512]{2,0,1:T(4,128)} %copy.8), calls=%async_computation.1 | async-start | bytes 1048576 | tf_op jit(solution)/shard_map/all_to_all | solution.py:87
  196.7 264.4 %all-reduce.36.cloned.1.call-start = ((), (), s32[]{:S(2)}) async-start(), calls=%async_computation.3 | async-start | bytes 524288 | tf_op jit(solution)/shard_map/psum | solution.py:99
  (7 other events, 299.0 us)
Sparse Core Ops, SparseCore 0:
  215.7 245.3 all-reduce.35
where the time goes:
time: 499 us; the launch traced here: 498 us
  waiting for transfers between devices  344 us (69%)
  starting transfers between devices  93 us (19%)
  blocking collectives  27.3 us (5%)
  between operations  14.1 us (3%)
  other arithmetic  10.8 us (2%)
  local copies, waits for them, and re-layouts  5.66 us (1%)
    psum x1, waiting for transfers between devices, on_device(): gram = lax.psum(partial_gram, ('dom', 'slab'))  245 us
    ppermute x16, waiting for transfers between devices, with_halo(): lax.ppermute(lax.slice_in_dim(block, 0, width, axis=dim), axis, backward)  57.2 us
    ppermute x16, starting transfers between devices, with_halo(): lax.ppermute(lax.slice_in_dim(block, block.shape[dim] - width, None, axis...  37 us
    all_to_all x1, starting transfers between devices, on_device(): lax.all_to_all(logperm.reshape(particles, -1), 'dom', split_axis=1, conca...  28.9 us
    all_to_all x1, blocking collectives, on_device(): lax.all_to_all(moved, 'dom', split_axis=0, concat_axis=1, tiled=True)  27.3 us
    ppermute x16, starting transfers between devices, with_halo(): lax.ppermute(lax.slice_in_dim(block, 0, width, axis=dim), axis, backward)  20.8 us
    all_to_all x1, waiting for transfers between devices, on_device(): lax.all_to_all(g_flat, 'dom', split_axis=1, concat_axis=0, tiled=True)  16.9 us
    all_to_all x1, waiting for transfers between devices, on_device(): lax.all_to_all(logperm.reshape(particles, -1), 'dom', split_axis=1, conca...  13.7 us
  transfers between devices with their start and end apart: 35, of which 33 were waited for; matrix products, arithmetic and copies ran while one was open for 1% of the time, Pallas kernels for 0%

commit v1 on v0

--- a/solution.py
+++ b/solution.py
@@ -110,7 +110,10 @@
             preferred_element_type=jnp.float32,
         )
     )
-    returned = lax.all_to_all(moved, "dom", split_axis=0, concat_axis=1, tiled=True)
+    size = lax.axis_size("dom")
+    pieces = jnp.stack(jnp.split(moved, size, axis=0), axis=0)
+    pieces = lax.all_to_all(pieces, "dom", split_axis=0, concat_axis=0)
+    returned = jnp.concatenate(pieces, axis=1)
     return returned.reshape(logperm.shape)
 
 

time: 499 us -> 500 us (level)
  no operation moved by 1% of the time
where the time goes in v1:
time: 500 us; the launch traced here: 499 us
  waiting for transfers between devices  344 us (69%)
  starting transfers between devices  93 us (19%)
  blocking collectives  27.3 us (5%)
  between operations  14.3 us (3%)
  other arithmetic  10.8 us (2%)
  local copies, waits for them, and re-layouts  6.16 us (1%)
    psum x1, waiting for transfers between devices, on_device(): gram = lax.psum(partial_gram, ('dom', 'slab'))  245 us
    ppermute x16, waiting for transfers between devices, with_halo(): lax.ppermute(lax.slice_in_dim(block, 0, width, axis=dim), axis, backward)  57.2 us
    ppermute x16, starting transfers between devices, with_halo(): lax.ppermute(lax.slice_in_dim(block, block.shape[dim] - width, None, axis...  37 us
    all_to_all x1, starting transfers between devices, on_device(): lax.all_to_all(logperm.reshape(particles, -1), 'dom', split_axis=1, conca...  28.9 us
    all_to_all x1, blocking collectives, on_device(): pieces = lax.all_to_all(pieces, 'dom', split_axis=0, concat_axis=0)  27.3 us
    ppermute x16, starting transfers between devices, with_halo(): lax.ppermute(lax.slice_in_dim(block, 0, width, axis=dim), axis, backward)  20.8 us
    all_to_all x1, waiting for transfers between devices, on_device(): lax.all_to_all(g_flat, 'dom', split_axis=1, concat_axis=0, tiled=True)  16.9 us
    all_to_all x1, waiting for transfers between devices, on_device(): lax.all_to_all(logperm.reshape(particles, -1), 'dom', split_axis=1, conca...  13.7 us
  transfers between devices with their start and end apart: 35, of which 33 were waited for; matrix products, arithmetic and copies ran while one was open for 1% of the time, Pallas kernels for 0%

profile of v1, /device:TPU:1, one launch (start us, length us, event | category | flops | bytes accessed | tf_op | source)
XLA Modules:
  0.0 498.8 jit_solution(8899087090216384197)
XLA Ops:
  7.6 4.0 collective-permute-start
  13.7 3.6 collective-permute-done.1
  18.9 3.2 collective-permute-start.2
  24.1 3.8 collective-permute-done.3
  28.3 2.9 collective-permute-start.4
  33.1 3.8 collective-permute-done.5
  37.3 2.2 collective-permute-start.6
  41.5 3.8 collective-permute-done.7
  45.6 1.9 collective-permute-start.8
  49.5 3.8 collective-permute-done.9
  57.5 3.8 collective-permute-done.11
  61.7 2.1 collective-permute-start.12
  66.1 4.1 collective-permute-done.13
  75.3 3.9 collective-permute-done.15
  79.7 2.1 collective-permute-start.16
  84.1 3.8 collective-permute-done.17
  88.4 2.2 collective-permute-start.18
  92.5 3.8 collective-permute-done.19
  96.8 2.2 collective-permute-start.20
  100.9 3.8 collective-permute-done.21
  105.2 2.2 collective-permute-start.22
  109.4 3.8 collective-permute-done.23
  117.5 3.8 collective-permute-done.25
  125.6 3.8 collective-permute-done.27
  133.8 3.9 collective-permute-done.29
  139.1 2.6 collective-permute-start.30
  144.2 28.9 %all-to-all-start = ((f32[4,64,512]{2,0,1:T(4,128)}), f32[4,64,512]{2,0,1:T(4,128)S(1)}, u32[]{:S(2)}, u32[]{:S(2)}) async-start(f32[4,64,512]{2,0,1:T(4,128)} %copy.6), calls=%async_computation | async-start | bytes 1048576 | tf_op jit(solution)/shard_map/all_to_all | solution.py:84
  176.8 13.7 %all-to-all-done = f32[4,64,512]{2,0,1:T(4,128)S(1)} async-done(((f32[4,64,512]{2,0,1:T(4,128)}), f32[4,64,512]{2,0,1:T(4,128)S(1)}, u32[]{:S(2)}, u32[]{:S(2)}) %all-to-all-start) | async-done | bytes 524320 | tf_op jit(solution)/shard_map/all_to_all | solution.py:84
  190.4 6.3 %all-to-all-start.1 = ((f32[4,64,512]{2,0,1:T(4,128)}), f32[4,64,512]{2,0,1:T(4,128)S(1)}, u32[]{:S(2)}, u32[]{:S(2)}) async-start(f32[4,64,512]{2,0,1:T(4,128)} %copy.7), calls=%async_computation.1 | async-start | bytes 1048576 | tf_op jit(solution)/shard_map/all_to_all | solution.py:87
  197.2 16.9 %all-to-all-done.1 = f32[4,64,512]{2,0,1:T(4,128)S(1)} async-done(((f32[4,64,512]{2,0,1:T(4,128)}), f32[4,64,512]{2,0,1:T(4,128)S(1)}, u32[]{:S(2)}, u32[]{:S(2)}) %all-to-all-start.1) | async-done | bytes 524320 | tf_op jit(solution)/shard_map/all_to_all | solution.py:87
  215.8 245.4 %all-reduce.36.cloned.1.call-done = f32[256,256]{1,0:T(8,128)} async-done(((f32[256,256]{1,0:T(8,128)}), f32[256,256]{1,0:T(8,128)}) %all-reduce.36.cloned.1.call-update) | async-done | bytes 262160 | tf_op jit(solution)/shard_map/psum | solution.py:99
  463.7 27.3 %all_to_all.43 = f32[64,4,512]{2,1,0:T(4,128)S(1)} all-to-all(f32[64,4,512]{2,1,0:T(4,128)S(1)} %constant_dynamic-update-slice_fusion), channel_id=1, replica_groups=mesh['dom'=64,'slab'=4] {'dom'}, dimensions={0} | all-to-all | bytes 1048576 | tf_op jit(solution)/shard_map/all_to_all | solution.py:115
  (162 shorter events, 61.3 us)
Async XLA Ops:
  7.6 6.2 %collective-permute-start = (f32[4,1,64,128]{3,2,1,0:T(8,128)S(1)}, f32[4,1,64,128]{3,2,1,0:T(8,128)S(1)}, u32[]{:S(2)}, u32[]{:S(2)}) collective-permute-start(f32[4,1,64,128]{3,2,1,0:T(8,128)S(1)} %get-tuple-element.41), channel_id=1, source_target_pairs={{0,1},{1,2},{2,3},{4,5},{5,6},{6,7},{8,9},{9,10},{10,11},{12,13},{... | collective-permute-start | bytes 393224 | tf_op jit(solution)/shard_map/ppermute | solution.py:16
  11.6 5.7 %collective-permute-start.1 = (f32[4,1,64,128]{3,2,1,0:T(8,128)S(1)}, f32[4,1,64,128]{3,2,1,0:T(8,128)S(1)}, u32[]{:S(2)}, u32[]{:S(2)}) collective-permute-start(f32[4,1,64,128]{3,2,1,0:T(8,128)S(1)} %get-tuple-element.42), channel_id=1, source_target_pairs={{1,0},{2,1},{3,2},{5,4},{6,5},{7,6},{9,8},{10,9},{11,10},{13,12},{... | collective-permute-start | bytes 393224 | tf_op jit(solution)/shard_map/ppermute | solution.py:19
  18.9 5.1 %collective-permute-start.2 = (f32[4,1,64,128]{3,2,1,0:T(8,128)S(1)}, f32[4,1,64,128]{3,2,1,0:T(8,128)S(1)}, u32[]{:S(2)}, u32[]{:S(2)}) collective-permute-start(f32[4,1,64,128]{3,2,1,0:T(8,128)S(1)} %get-tuple-element.39), channel_id=1, source_target_pairs={{0,1},{1,2},{2,3},{4,5},{5,6},{6,7},{8,9},{9,10},{10,11},{12,13},{... | collective-permute-start | bytes 393224 | tf_op jit(solution)/shard_map/ppermute | solution.py:16
  22.2 5.7 %collective-permute-start.3 = (f32[4,1,64,128]{3,2,1,0:T(8,128)S(1)}, f32[4,1,64,128]{3,2,1,0:T(8,128)S(1)}, u32[]{:S(2)}, u32[]{:S(2)}) collective-permute-start(f32[4,1,64,128]{3,2,1,0:T(8,128)S(1)} %get-tuple-element.40), channel_id=1, source_target_pairs={{1,0},{2,1},{3,2},{5,4},{6,5},{7,6},{9,8},{10,9},{11,10},{13,12},{... | collective-permute-start | bytes 393224 | tf_op jit(solution)/shard_map/ppermute | solution.py:19
  28.3 4.8 collective-permute-start.4
  31.2 5.7 %collective-permute-start.5 = (f32[4,1,64,128]{3,2,1,0:T(8,128)S(1)}, f32[4,1,64,128]{3,2,1,0:T(8,128)S(1)}, u32[]{:S(2)}, u32[]{:S(2)}) collective-permute-start(f32[4,1,64,128]{3,2,1,0:T(8,128)S(1)} %get-tuple-element.38), channel_id=1, source_target_pairs={{1,0},{2,1},{3,2},{5,4},{6,5},{7,6},{9,8},{10,9},{11,10},{13,12},{... | collective-permute-start | bytes 393224 | tf_op jit(solution)/shard_map/ppermute | solution.py:19
  37.3 4.1 collective-permute-start.6
  39.5 5.7 %collective-permute-start.7 = (f32[4,1,64,128]{3,2,1,0:T(8,128)S(1)}, f32[4,1,64,128]{3,2,1,0:T(8,128)S(1)}, u32[]{:S(2)}, u32[]{:S(2)}) collective-permute-start(f32[4,1,64,128]{3,2,1,0:T(8,128)S(1)} %get-tuple-element.36), channel_id=1, source_target_pairs={{1,0},{2,1},{3,2},{5,4},{6,5},{7,6},{9,8},{10,9},{11,10},{13,12},{... | collective-permute-start | bytes 393224 | tf_op jit(solution)/shard_map/ppermute | solution.py:19
  45.6 3.9 collective-permute-start.8
  47.6 5.7 %collective-permute-start.9 = (f32[4,1,64,128]{3,2,1,0:T(8,128)S(1)}, f32[4,1,64,128]{3,2,1,0:T(8,128)S(1)}, u32[]{:S(2)}, u32[]{:S(2)}) collective-permute-start(f32[4,1,64,128]{3,2,1,0:T(8,128)S(1)} %get-tuple-element.34), channel_id=1, source_target_pairs={{1,0},{2,1},{3,2},{5,4},{6,5},{7,6},{9,8},{10,9},{11,10},{13,12},{... | collective-permute-start | bytes 393224 | tf_op jit(solution)/shard_map/ppermute | solution.py:19
  53.7 3.9 collective-permute-start.10
  55.6 5.7 %collective-permute-start.11 = (f32[4,1,64,128]{3,2,1,0:T(8,128)S(1)}, f32[4,1,64,128]{3,2,1,0:T(8,128)S(1)}, u32[]{:S(2)}, u32[]{:S(2)}) collective-permute-start(f32[4,1,64,128]{3,2,1,0:T(8,128)S(1)} %get-tuple-element.32), channel_id=1, source_target_pairs={{1,0},{2,1},{3,2},{5,4},{6,5},{7,6},{9,8},{10,9},{11,10},{13,12},{... | collective-permute-start | bytes 393224 | tf_op jit(solution)/shard_map/ppermute | solution.py:19
  61.7 4.3 collective-permute-start.12
  63.8 6.4 %collective-permute-start.13 = (f32[4,1,64,128]{3,2,1,0:T(8,128)S(1)}, f32[4,1,64,128]{3,2,1,0:T(8,128)S(1)}, u32[]{:S(2)}, u32[]{:S(2)}) collective-permute-start(f32[4,1,64,128]{3,2,1,0:T(8,128)S(1)} %get-tuple-element.30), channel_id=1, source_target_pairs={{1,0},{2,1},{3,2},{5,4},{6,5},{7,6},{9,8},{10,9},{11,10},{13,12},{... | collective-permute-start | bytes 393224 | tf_op jit(solution)/shard_map/ppermute | solution.py:19
  70.6 4.7 collective-permute-start.14
  72.2 7.0 %collective-permute-start.15 = (f32[4,1,64,128]{3,2,1,0:T(8,128)S(1)}, f32[4,1,64,128]{3,2,1,0:T(8,128)S(1)}, u32[]{:S(2)}, u32[]{:S(2)}) collective-permute-start(f32[4,1,64,128]{3,2,1,0:T(8,128)S(1)} %get-tuple-element.28), channel_id=1, source_target_pairs={{1,0},{2,1},{3,2},{5,4},{6,5},{7,6},{9,8},{10,9},{11,10},{13,12},{... | collective-permute-start | bytes 393224 | tf_op jit(solution)/shard_map/ppermute | solution.py:19
  79.7 4.4 collective-permute-start.16
  81.8 6.1 %collective-permute-start.17 = (f32[4,1,64,128]{3,2,1,0:T(8,128)S(1)}, f32[4,1,64,128]{3,2,1,0:T(8,128)S(1)}, u32[]{:S(2)}, u32[]{:S(2)}) collective-permute-start(f32[4,1,64,128]{3,2,1,0:T(8,128)S(1)} %get-tuple-element.26), channel_id=1, source_target_pairs={{1,0},{2,1},{3,2},{5,4},{6,5},{7,6},{9,8},{10,9},{11,10},{13,12},{... | collective-permute-start | bytes 393224 | tf_op jit(solution)/shard_map/ppermute | solution.py:19
  88.4 4.2 collective-permute-start.18
  90.6 5.7 %collective-permute-start.19 = (f32[4,1,64,128]{3,2,1,0:T(8,128)S(1)}, f32[4,1,64,128]{3,2,1,0:T(8,128)S(1)}, u32[]{:S(2)}, u32[]{:S(2)}) collective-permute-start(f32[4,1,64,128]{3,2,1,0:T(8,128)S(1)} %get-tuple-element.24), channel_id=1, source_target_pairs={{1,0},{2,1},{3,2},{5,4},{6,5},{7,6},{9,8},{10,9},{11,10},{13,12},{... | collective-permute-start | bytes 393224 | tf_op jit(solution)/shard_map/ppermute | solution.py:19
  96.8 4.1 collective-permute-start.20
  99.0 5.7 %collective-permute-start.21 = (f32[4,1,64,128]{3,2,1,0:T(8,128)S(1)}, f32[4,1,64,128]{3,2,1,0:T(8,128)S(1)}, u32[]{:S(2)}, u32[]{:S(2)}) collective-permute-start(f32[4,1,64,128]{3,2,1,0:T(8,128)S(1)} %get-tuple-element.22), channel_id=1, source_target_pairs={{1,0},{2,1},{3,2},{5,4},{6,5},{7,6},{9,8},{10,9},{11,10},{13,12},{... | collective-permute-start | bytes 393224 | tf_op jit(solution)/shard_map/ppermute | solution.py:19
  105.2 4.1 collective-permute-start.22
  107.4 5.7 %collective-permute-start.23 = (f32[4,1,64,128]{3,2,1,0:T(8,128)S(1)}, f32[4,1,64,128]{3,2,1,0:T(8,128)S(1)}, u32[]{:S(2)}, u32[]{:S(2)}) collective-permute-start(f32[4,1,64,128]{3,2,1,0:T(8,128)S(1)} %get-tuple-element.20), channel_id=1, source_target_pairs={{1,0},{2,1},{3,2},{5,4},{6,5},{7,6},{9,8},{10,9},{11,10},{13,12},{... | collective-permute-start | bytes 393224 | tf_op jit(solution)/shard_map/ppermute | solution.py:19
  115.6 5.7 %collective-permute-start.25 = (f32[4,1,64,128]{3,2,1,0:T(8,128)S(1)}, f32[4,1,64,128]{3,2,1,0:T(8,128)S(1)}, u32[]{:S(2)}, u32[]{:S(2)}) collective-permute-start(f32[4,1,64,128]{3,2,1,0:T(8,128)S(1)} %get-tuple-element.18), channel_id=1, source_target_pairs={{1,0},{2,1},{3,2},{5,4},{6,5},{7,6},{9,8},{10,9},{11,10},{13,12},{... | collective-permute-start | bytes 393224 | tf_op jit(solution)/shard_map/ppermute | solution.py:19
  123.7 5.7 %collective-permute-start.27 = (f32[4,1,64,128]{3,2,1,0:T(8,128)S(1)}, f32[4,1,64,128]{3,2,1,0:T(8,128)S(1)}, u32[]{:S(2)}, u32[]{:S(2)}) collective-permute-start(f32[4,1,64,128]{3,2,1,0:T(8,128)S(1)} %get-tuple-element.16), channel_id=1, source_target_pairs={{1,0},{2,1},{3,2},{5,4},{6,5},{7,6},{9,8},{10,9},{11,10},{13,12},{... | collective-permute-start | bytes 393224 | tf_op jit(solution)/shard_map/ppermute | solution.py:19
  131.9 5.8 %collective-permute-start.29 = (f32[4,1,64,128]{3,2,1,0:T(8,128)S(1)}, f32[4,1,64,128]{3,2,1,0:T(8,128)S(1)}, u32[]{:S(2)}, u32[]{:S(2)}) collective-permute-start(f32[4,1,64,128]{3,2,1,0:T(8,128)S(1)} %get-tuple-element.14), channel_id=1, source_target_pairs={{1,0},{2,1},{3,2},{5,4},{6,5},{7,6},{9,8},{10,9},{11,10},{13,12},{... | collective-permute-start | bytes 393224 | tf_op jit(solution)/shard_map/ppermute | solution.py:19
  139.1 34.1 %collective-permute-start.30 = (f32[2,4,1,64,128]{4,3,2,1,0:T(8,128)}, f32[2,4,1,64,128]{4,3,2,1,0:T(8,128)}, u32[]{:S(2)}, u32[]{:S(2)}) collective-permute-start(f32[2,4,1,64,128]{4,3,2,1,0:T(8,128)} %get-tuple-element.11), channel_id=1, source_target_pairs={{0,1},{1,2},{2,3},{4,5},{5,6},{6,7},{8,9},{9,10},{10,11},{12,13},{... | collective-permute-start | bytes 786440 | tf_op jit(solution)/shard_map/ppermute | solution.py:16
  141.7 31.5 %collective-permute-start.31 = (f32[2,4,1,64,128]{4,3,2,1,0:T(8,128)}, f32[2,4,1,64,128]{4,3,2,1,0:T(8,128)}, u32[]{:S(2)}, u32[]{:S(2)}) collective-permute-start(f32[2,4,1,64,128]{4,3,2,1,0:T(8,128)} %get-tuple-element.12), channel_id=1, source_target_pairs={{1,0},{2,1},{3,2},{5,4},{6,5},{7,6},{9,8},{10,9},{11,10},{13,12},{... | collective-permute-start | bytes 786440 | tf_op jit(solution)/shard_map/ppermute | solution.py:19
  144.2 46.3 %all-to-all-start = ((f32[4,64,512]{2,0,1:T(4,128)}), f32[4,64,512]{2,0,1:T(4,128)S(1)}, u32[]{:S(2)}, u32[]{:S(2)}) async-start(f32[4,64,512]{2,0,1:T(4,128)} %copy.6), calls=%async_computation | async-start | bytes 1048576 | tf_op jit(solution)/shard_map/all_to_all | solution.py:84
  190.4 23.6 %all-to-all-start.1 = ((f32[4,64,512]{2,0,1:T(4,128)}), f32[4,64,512]{2,0,1:T(4,128)S(1)}, u32[]{:S(2)}, u32[]{:S(2)}) async-start(f32[4,64,512]{2,0,1:T(4,128)} %copy.7), calls=%async_computation.1 | async-start | bytes 1048576 | tf_op jit(solution)/shard_map/all_to_all | solution.py:87
  196.7 264.5 %all-reduce.36.cloned.1.call-start = ((), (), s32[]{:S(2)}) async-start(), calls=%async_computation.3 | async-start | bytes 524288 | tf_op jit(solution)/shard_map/psum | solution.py:99
  (7 other events, 299.1 us)
Sparse Core Ops, SparseCore 0:
  215.7 245.4 all-reduce.35
